TPU v7x, 32 devices: a whole 2x2x4 slice. The times are simulated.
32 devices in a mesh: row: 8 (over y, x, core), col: 4 (over z).
Axes of the slice: x: 2, y: 2, z: 4, core: 2. Of those that a mesh axis runs over, the one named last changes fastest.
Arguments:
- left_panels: float32 [8, 4, 16, 128, 128], P('row', 'col'), may hold values from -6 to 6
- right_panels: float32 [2, 4, 8, 12, 128, 128], P(None, 'col', 'row'), may hold values from -0.25 to 0.25
- product_lists: int32 [8, 4, 8, 96, 3], P('row', 'col'), may hold values from -1 to 23, as said below
Outputs:
- product_blocks: float32 [8, 4, 24, 128, 128], P('row', 'col')
Inputs may be any that keep to these rules, and one draw needn't show every extreme that they name: `product_lists`: each entry is (left slot < 16, right slot < 12, output slot < 24). In each list the first entries, at least half of 96 and at most 96, are live with distinct (left, right) pairs, the rest are -1 in all three columns; some list holds 96 live entries.
All inputs are finite; a program needn't handle non-finite values.
Results may differ from a plain program's by a relative error of at most 0.0003.
Values sent between devices are 32-bit elements; how exact they have to be, the bound alone decides.
A program may use at most 128 MiB of HBM per device.

v0:
```python
import jax
import jax.numpy as jnp
from jax import lax
from jax.sharding import PartitionSpec as P

BLK = 128
OCAP = 24


def contribute(left_stack, right_panel, entries, slot_count):
    live_mask = entries[:, 0] >= 0
    left_slot = jnp.maximum(entries[:, 0], 0)
    right_slot = jnp.maximum(entries[:, 1], 0)
    taken_left = jnp.take(left_stack, left_slot, axis=0)
    taken_right = jnp.take(right_panel, right_slot, axis=0)
    blocks = jnp.einsum("pik,pkj->pij", taken_left, taken_right, precision=lax.Precision.HIGHEST)
    slot_ids = jnp.arange(slot_count, dtype=jnp.int32)
    onehot = ((entries[:, 2][None, :] == slot_ids[:, None]) & live_mask[None, :]).astype(
        blocks.dtype
    )
    return jnp.einsum("op,pij->oij", onehot, blocks, precision=lax.Precision.HIGHEST)


def shards(left_panels, right_panels, product_lists):
    row_count = lax.axis_size("row")
    col_count = lax.axis_size("col")
    row_pos = lax.axis_index("row")
    col_pos = lax.axis_index("col")
    entries = product_lists[0, 0]
    step_count = entries.shape[0]
    running = jnp.zeros((OCAP, BLK, BLK), jnp.float32)
    right_all = lax.all_gather(right_panels, "col", axis=1, tiled=True)
    pieces = lax.all_gather(left_panels, "row", axis=0, tiled=True)

    def one_row(offset, partial_value):
        step_num = (offset - row_pos - col_pos) % row_count
        left_stack = lax.dynamic_index_in_dim(pieces, offset, 0, keepdims=False)[0]
        right_panel = right_all[offset // col_count, offset % col_count, 0]
        entry_rows = lax.dynamic_index_in_dim(
            entries, jnp.minimum(step_num, step_count - 1), 0, keepdims=False
        )
        return lax.cond(
            step_num < step_count,
            lambda inner: inner + contribute(left_stack, right_panel, entry_rows, OCAP),
            lambda inner: inner,
            partial_value,
        )

    running = lax.fori_loop(0, pieces.shape[0], one_row, running)
    return running[None, None]


def solution(mesh):
    return jax.shard_map(
        shards,
        mesh=mesh,
        in_specs=(
            P("row", "col", None, None, None),
            P(None, "col", "row", None, None, None),
            P("row", "col", None, None, None),
        ),
        out_specs=P("row", "col", None, None, None),
        check_vma=False,
    )
```

profile of v0, /device:TPU:0, one launch (start us, length us, event | category | flops | bytes accessed | tf_op | source)
XLA Modules:
  0.0 394.5 jit_solution(15243626719083775768)
XLA Ops:
  8.7 118.3 %all-gather.5.cloned.1.call-done = f32[2,4,1,12,128,128]{5,4,3,2,1,0:T(8,128)} async-done(((f32[2,1,1,12,128,128]{5,4,3,2,1,0:T(8,128)}), f32[2,4,1,12,128,128]{5,4,3,2,1,0:T(8,128)}) %all-gather.5.cloned.1.call-update) | async-done | bytes 6291472 | tf_op jit(solution)/shard_map/all_gather | solution.py:32
  127.0 54.4 %all-gather.3.cloned.1.call-done = f32[8,1,16,128,128]{4,3,2,1,0:T(8,128)} async-done(((f32[1,1,16,128,128]{4,3,2,1,0:T(8,128)}), f32[8,1,16,128,128]{4,3,2,1,0:T(8,128)}) %all-gather.3.cloned.1.call-update) | async-done | bytes 8388624 | tf_op jit(solution)/shard_map/all_gather | solution.py:33
  181.5 204.8 %while.19 = (s32[]{:T(128)}, f32[24,128,128]{2,0,1:T(8,128)S(1)}, s32[]{:T(128)}, s32[]{:T(128)}, s32[8,96,3]{1,2,0:T(4,128)S(1)}, /*index=5*/f32[8,1,16,128,128...) while((s32[]{:T(128)}, f32[24,128,128]{2,0,1:T(8,128)S(1)}, ...), condition=%wide.region_3.4_spmd, body=%wide.region_0.3_spmd.sunk | while | flops 2872450304 | bytes 57164012 | solution.py:49
  181.5 25.6 %conditional.2 = (f32[24,128,128]{2,0,1:T(8,128)S(1)}) conditional(s32[]{:T(128)} %convert_element_type.13, f32[24,128,128]{2,0,1:T(8,128)S(1)} %get-tuple-element.574, (s32[]{:T(128)}, s32[8,96,3]{1,2,0:T(4,128)S(1)}, s32[]{:T(128)}, f32[8,1,16,128,128]{4,3,2,1,0:T(8,128)}, f32[2,4,1,12,128,128]{5,4,3,2,1,0:T(8,128)}, ...), branch_computations={%region_1.1_spmd, %region_2.2_spmd} | conditional | flops 2872450304 | bytes 57163708 | solution.py:42
  191.2 9.5 %fusion.2 = f32[96,128,128]{2,1,0:T(8,128)S(1)} fusion(f32[96,128,128]{2,1,0:T(8,128)} %gather_fusion.1, f32[96,128,128]{2,1,0:T(8,128)} %gather_fusion, pred[96]{0:T(512)(128)(4,1)S(1)} %get-tuple-element.513, pred[96]{0:T(512)(128)(4,1)S(1)} %get-tuple-element.512), kind=kOutput, calls=%fused_computation.4 | convolution fusion | flops 2419064832 | bytes 18874560 | tf_op jit(solution)/shard_map/while/body/eval_jaxpr/cond/branch_1_fun/pik,pkj->pij/dot_general | solution.py:16
  207.1 25.6 %conditional.2 = (f32[24,128,128]{2,0,1:T(8,128)S(1)}) conditional(s32[]{:T(128)} %convert_element_type.13, f32[24,128,128]{2,0,1:T(8,128)S(1)} %get-tuple-element.574, (s32[]{:T(128)}, s32[8,96,3]{1,2,0:T(4,128)S(1)}, s32[]{:T(128)}, f32[8,1,16,128,128]{4,3,2,1,0:T(8,128)}, f32[2,4,1,12,128,128]{5,4,3,2,1,0:T(8,128)}, ...), branch_computations={%region_1.1_spmd, %region_2.2_spmd} | conditional | flops 2872450304 | bytes 57163708 | solution.py:42
  216.8 9.5 %fusion.2 = f32[96,128,128]{2,1,0:T(8,128)S(1)} fusion(f32[96,128,128]{2,1,0:T(8,128)} %gather_fusion.1, f32[96,128,128]{2,1,0:T(8,128)} %gather_fusion, pred[96]{0:T(512)(128)(4,1)S(1)} %get-tuple-element.513, pred[96]{0:T(512)(128)(4,1)S(1)} %get-tuple-element.512), kind=kOutput, calls=%fused_computation.4 | convolution fusion | flops 2419064832 | bytes 18874560 | tf_op jit(solution)/shard_map/while/body/eval_jaxpr/cond/branch_1_fun/pik,pkj->pij/dot_general | solution.py:16
  226.4 6.3 %fusion.8 = f32[24,128,128]{2,0,1:T(8,128)S(1)} fusion(f32[24,128,128]{2,0,1:T(8,128)S(1)} %get-tuple-element.481, f32[96,128,128]{2,1,0:T(8,128)S(1)} %fusion.2, s32[96]{0:T(128)S(1)} %get-tuple-element.514, pred[96]{0:T(512)(128)(4,1)S(1)} %get-tuple-element.511), kind=kOutput, calls=%fused_computation.10 | convolution fusion | flops 453382656 | bytes 9437664 | tf_op jit(solution)/shard_map/while/body/eval_jaxpr/cond/branch_1_fun/op,pij->oij/dot_general | solution.py:21
  232.7 25.6 %conditional.2 = (f32[24,128,128]{2,0,1:T(8,128)S(1)}) conditional(s32[]{:T(128)} %convert_element_type.13, f32[24,128,128]{2,0,1:T(8,128)S(1)} %get-tuple-element.574, (s32[]{:T(128)}, s32[8,96,3]{1,2,0:T(4,128)S(1)}, s32[]{:T(128)}, f32[8,1,16,128,128]{4,3,2,1,0:T(8,128)}, f32[2,4,1,12,128,128]{5,4,3,2,1,0:T(8,128)}, ...), branch_computations={%region_1.1_spmd, %region_2.2_spmd} | conditional | flops 2872450304 | bytes 57163708 | solution.py:42
  242.4 9.5 %fusion.2 = f32[96,128,128]{2,1,0:T(8,128)S(1)} fusion(f32[96,128,128]{2,1,0:T(8,128)} %gather_fusion.1, f32[96,128,128]{2,1,0:T(8,128)} %gather_fusion, pred[96]{0:T(512)(128)(4,1)S(1)} %get-tuple-element.513, pred[96]{0:T(512)(128)(4,1)S(1)} %get-tuple-element.512), kind=kOutput, calls=%fused_computation.4 | convolution fusion | flops 2419064832 | bytes 18874560 | tf_op jit(solution)/shard_map/while/body/eval_jaxpr/cond/branch_1_fun/pik,pkj->pij/dot_general | solution.py:16
  252.0 6.3 %fusion.8 = f32[24,128,128]{2,0,1:T(8,128)S(1)} fusion(f32[24,128,128]{2,0,1:T(8,128)S(1)} %get-tuple-element.481, f32[96,128,128]{2,1,0:T(8,128)S(1)} %fusion.2, s32[96]{0:T(128)S(1)} %get-tuple-element.514, pred[96]{0:T(512)(128)(4,1)S(1)} %get-tuple-element.511), kind=kOutput, calls=%fused_computation.10 | convolution fusion | flops 453382656 | bytes 9437664 | tf_op jit(solution)/shard_map/while/body/eval_jaxpr/cond/branch_1_fun/op,pij->oij/dot_general | solution.py:21
  258.3 25.6 %conditional.2 = (f32[24,128,128]{2,0,1:T(8,128)S(1)}) conditional(s32[]{:T(128)} %convert_element_type.13, f32[24,128,128]{2,0,1:T(8,128)S(1)} %get-tuple-element.574, (s32[]{:T(128)}, s32[8,96,3]{1,2,0:T(4,128)S(1)}, s32[]{:T(128)}, f32[8,1,16,128,128]{4,3,2,1,0:T(8,128)}, f32[2,4,1,12,128,128]{5,4,3,2,1,0:T(8,128)}, ...), branch_computations={%region_1.1_spmd, %region_2.2_spmd} | conditional | flops 2872450304 | bytes 57163708 | solution.py:42
  268.0 9.5 %fusion.2 = f32[96,128,128]{2,1,0:T(8,128)S(1)} fusion(f32[96,128,128]{2,1,0:T(8,128)} %gather_fusion.1, f32[96,128,128]{2,1,0:T(8,128)} %gather_fusion, pred[96]{0:T(512)(128)(4,1)S(1)} %get-tuple-element.513, pred[96]{0:T(512)(128)(4,1)S(1)} %get-tuple-element.512), kind=kOutput, calls=%fused_computation.4 | convolution fusion | flops 2419064832 | bytes 18874560 | tf_op jit(solution)/shard_map/while/body/eval_jaxpr/cond/branch_1_fun/pik,pkj->pij/dot_general | solution.py:16
  277.6 6.3 %fusion.8 = f32[24,128,128]{2,0,1:T(8,128)S(1)} fusion(f32[24,128,128]{2,0,1:T(8,128)S(1)} %get-tuple-element.481, f32[96,128,128]{2,1,0:T(8,128)S(1)} %fusion.2, s32[96]{0:T(128)S(1)} %get-tuple-element.514, pred[96]{0:T(512)(128)(4,1)S(1)} %get-tuple-element.511), kind=kOutput, calls=%fused_computation.10 | convolution fusion | flops 453382656 | bytes 9437664 | tf_op jit(solution)/shard_map/while/body/eval_jaxpr/cond/branch_1_fun/op,pij->oij/dot_general | solution.py:21
  283.9 25.6 %conditional.2 = (f32[24,128,128]{2,0,1:T(8,128)S(1)}) conditional(s32[]{:T(128)} %convert_element_type.13, f32[24,128,128]{2,0,1:T(8,128)S(1)} %get-tuple-element.574, (s32[]{:T(128)}, s32[8,96,3]{1,2,0:T(4,128)S(1)}, s32[]{:T(128)}, f32[8,1,16,128,128]{4,3,2,1,0:T(8,128)}, f32[2,4,1,12,128,128]{5,4,3,2,1,0:T(8,128)}, ...), branch_computations={%region_1.1_spmd, %region_2.2_spmd} | conditional | flops 2872450304 | bytes 57163708 | solution.py:42
  293.6 9.5 %fusion.2 = f32[96,128,128]{2,1,0:T(8,128)S(1)} fusion(f32[96,128,128]{2,1,0:T(8,128)} %gather_fusion.1, f32[96,128,128]{2,1,0:T(8,128)} %gather_fusion, pred[96]{0:T(512)(128)(4,1)S(1)} %get-tuple-element.513, pred[96]{0:T(512)(128)(4,1)S(1)} %get-tuple-element.512), kind=kOutput, calls=%fused_computation.4 | convolution fusion | flops 2419064832 | bytes 18874560 | tf_op jit(solution)/shard_map/while/body/eval_jaxpr/cond/branch_1_fun/pik,pkj->pij/dot_general | solution.py:16
  303.2 6.3 %fusion.8 = f32[24,128,128]{2,0,1:T(8,128)S(1)} fusion(f32[24,128,128]{2,0,1:T(8,128)S(1)} %get-tuple-element.481, f32[96,128,128]{2,1,0:T(8,128)S(1)} %fusion.2, s32[96]{0:T(128)S(1)} %get-tuple-element.514, pred[96]{0:T(512)(128)(4,1)S(1)} %get-tuple-element.511), kind=kOutput, calls=%fused_computation.10 | convolution fusion | flops 453382656 | bytes 9437664 | tf_op jit(solution)/shard_map/while/body/eval_jaxpr/cond/branch_1_fun/op,pij->oij/dot_general | solution.py:21
  309.5 25.6 %conditional.2 = (f32[24,128,128]{2,0,1:T(8,128)S(1)}) conditional(s32[]{:T(128)} %convert_element_type.13, f32[24,128,128]{2,0,1:T(8,128)S(1)} %get-tuple-element.574, (s32[]{:T(128)}, s32[8,96,3]{1,2,0:T(4,128)S(1)}, s32[]{:T(128)}, f32[8,1,16,128,128]{4,3,2,1,0:T(8,128)}, f32[2,4,1,12,128,128]{5,4,3,2,1,0:T(8,128)}, ...), branch_computations={%region_1.1_spmd, %region_2.2_spmd} | conditional | flops 2872450304 | bytes 57163708 | solution.py:42
  319.2 9.5 %fusion.2 = f32[96,128,128]{2,1,0:T(8,128)S(1)} fusion(f32[96,128,128]{2,1,0:T(8,128)} %gather_fusion.1, f32[96,128,128]{2,1,0:T(8,128)} %gather_fusion, pred[96]{0:T(512)(128)(4,1)S(1)} %get-tuple-element.513, pred[96]{0:T(512)(128)(4,1)S(1)} %get-tuple-element.512), kind=kOutput, calls=%fused_computation.4 | convolution fusion | flops 2419064832 | bytes 18874560 | tf_op jit(solution)/shard_map/while/body/eval_jaxpr/cond/branch_1_fun/pik,pkj->pij/dot_general | solution.py:16
  328.8 6.3 %fusion.8 = f32[24,128,128]{2,0,1:T(8,128)S(1)} fusion(f32[24,128,128]{2,0,1:T(8,128)S(1)} %get-tuple-element.481, f32[96,128,128]{2,1,0:T(8,128)S(1)} %fusion.2, s32[96]{0:T(128)S(1)} %get-tuple-element.514, pred[96]{0:T(512)(128)(4,1)S(1)} %get-tuple-element.511), kind=kOutput, calls=%fused_computation.10 | convolution fusion | flops 453382656 | bytes 9437664 | tf_op jit(solution)/shard_map/while/body/eval_jaxpr/cond/branch_1_fun/op,pij->oij/dot_general | solution.py:21
  335.1 25.6 %conditional.2 = (f32[24,128,128]{2,0,1:T(8,128)S(1)}) conditional(s32[]{:T(128)} %convert_element_type.13, f32[24,128,128]{2,0,1:T(8,128)S(1)} %get-tuple-element.574, (s32[]{:T(128)}, s32[8,96,3]{1,2,0:T(4,128)S(1)}, s32[]{:T(128)}, f32[8,1,16,128,128]{4,3,2,1,0:T(8,128)}, f32[2,4,1,12,128,128]{5,4,3,2,1,0:T(8,128)}, ...), branch_computations={%region_1.1_spmd, %region_2.2_spmd} | conditional | flops 2872450304 | bytes 57163708 | solution.py:42
  344.8 9.5 %fusion.2 = f32[96,128,128]{2,1,0:T(8,128)S(1)} fusion(f32[96,128,128]{2,1,0:T(8,128)} %gather_fusion.1, f32[96,128,128]{2,1,0:T(8,128)} %gather_fusion, pred[96]{0:T(512)(128)(4,1)S(1)} %get-tuple-element.513, pred[96]{0:T(512)(128)(4,1)S(1)} %get-tuple-element.512), kind=kOutput, calls=%fused_computation.4 | convolution fusion | flops 2419064832 | bytes 18874560 | tf_op jit(solution)/shard_map/while/body/eval_jaxpr/cond/branch_1_fun/pik,pkj->pij/dot_general | solution.py:16
  360.7 25.6 %conditional.2 = (f32[24,128,128]{2,0,1:T(8,128)S(1)}) conditional(s32[]{:T(128)} %convert_element_type.13, f32[24,128,128]{2,0,1:T(8,128)S(1)} %get-tuple-element.574, (s32[]{:T(128)}, s32[8,96,3]{1,2,0:T(4,128)S(1)}, s32[]{:T(128)}, f32[8,1,16,128,128]{4,3,2,1,0:T(8,128)}, f32[2,4,1,12,128,128]{5,4,3,2,1,0:T(8,128)}, ...), branch_computations={%region_1.1_spmd, %region_2.2_spmd} | conditional | flops 2872450304 | bytes 57163708 | solution.py:42
  370.4 9.5 %fusion.2 = f32[96,128,128]{2,1,0:T(8,128)S(1)} fusion(f32[96,128,128]{2,1,0:T(8,128)} %gather_fusion.1, f32[96,128,128]{2,1,0:T(8,128)} %gather_fusion, pred[96]{0:T(512)(128)(4,1)S(1)} %get-tuple-element.513, pred[96]{0:T(512)(128)(4,1)S(1)} %get-tuple-element.512), kind=kOutput, calls=%fused_computation.4 | convolution fusion | flops 2419064832 | bytes 18874560 | tf_op jit(solution)/shard_map/while/body/eval_jaxpr/cond/branch_1_fun/pik,pkj->pij/dot_general | solution.py:16
  (74 shorter events, 99.7 us)
Async XLA Ops:
  6.5 120.4 %all-gather.5.cloned.1.call-start = ((), (), s32[]{:S(2)}) async-start(), calls=%async_computation.1 | async-start | bytes 7864320 | tf_op jit(solution)/shard_map/all_gather | solution.py:32
  7.3 174.1 %all-gather.3.cloned.1.call-start = ((), (), s32[]{:S(2)}) async-start(), calls=%async_computation | async-start | bytes 9437184 | tf_op jit(solution)/shard_map/all_gather | solution.py:33
Sparse Core Ops, SparseCore 0:
  8.9 118.0 all-gather.4
  128.9 52.4 all-gather.2
where the time goes:
time: 395 us
  waiting for transfers between devices  174 us (44%)
  matrix products  127 us (32%)
  local copies, waits for them, and re-layouts  79.3 us (20%)
  between operations  13.4 us (3%)
    all_gather x1, waiting for transfers between devices, shards(): right_all = lax.all_gather(right_panels, 'col', axis=1, tiled=True)  118 us
    dot_general x8, matrix products, contribute(): jnp.einsum('pik,pkj->pij', taken_left, taken_right, precision=lax.Precisi...  76.2 us
    all_gather x1, waiting for transfers between devices, shards(): pieces = lax.all_gather(left_panels, 'row', axis=0, tiled=True)  54.4 us
    dot_general x8, matrix products, contribute(): jnp.einsum('op,pij->oij', onehot, blocks, precision=lax.Precision.HIGHEST)  50.3 us
    gather x8, local copies, waits for them, and re-layouts, contribute(): taken_left = jnp.take(left_stack, left_slot, axis=0)  28.9 us
    gather x8, local copies, waits for them, and re-layouts, contribute(): taken_right = jnp.take(right_panel, right_slot, axis=0)  28.2 us
    squeeze x8, local copies, waits for them, and re-layouts, one_row(): left_stack = lax.dynamic_index_in_dim(pieces, offset, 0, keepdims=False)[0]  10.3 us
    squeeze x8, local copies, waits for them, and re-layouts, one_row(): right_panel = right_all[offset // col_count, offset % col_count, 0]  9.53 us
  transfers between devices with their start and end apart: 2, of which 2 were waited for; matrix products, arithmetic and copies ran while one was open for 0% of the time, Pallas kernels for 0%

commit v1 on v0

--- a/solution.py
+++ b/solution.py
@@ -29,7 +29,14 @@
     entries = product_lists[0, 0]
     step_count = entries.shape[0]
     running = jnp.zeros((OCAP, BLK, BLK), jnp.float32)
-    right_all = lax.all_gather(right_panels, "col", axis=1, tiled=True)
+    x = right_panels
+    ways, here, turn = (lax.axis_size("col"), lax.axis_index("col"), x.shape[1])
+    shape = [n * ways if d == 1 else n for d, n in enumerate(x.shape)]
+    full = lax.dynamic_update_slice_in_dim(jnp.zeros(shape, x.dtype), x, here * turn, axis=1)
+    for far in range(1, ways):
+        x = lax.ppermute(x, "col", [(d, (d + 1) % ways) for d in range(ways)])
+        full = lax.dynamic_update_slice_in_dim(full, x, (here - far) % ways * turn, axis=1)
+    right_all = full
     pieces = lax.all_gather(left_panels, "row", axis=0, tiled=True)
 
     def one_row(offset, partial_value):

time: 395 us -> 338 us (0.86)
  waiting for transfers between devices: 174 us -> 102 us
  local copies, waits for them, and re-layouts: 79.3 us -> 90.9 us
    all_gather x1 -> x0, waiting for transfers between devices: 118 us -> none  [shards(): right_all = lax.all_gather(right_panels, 'col', axis=1, tiled=True)]
    ppermute x0 -> x3, waiting for transfers between devices: none -> 102 us  [shards(): x = lax.ppermute(x, 'col', [(d, (d + 1) % ways) for d in range(ways)])]
    all_gather x1, waiting for transfers between devices: 54.4 us -> 0.01 us  [shards(): pieces = lax.all_gather(left_panels, 'row', axis=0, tiled=True)]
    dynamic_update_slice x0 -> x4, local copies, waits for them, and re-layouts: none -> 7.99 us  [the longest x3 6.72 us: shards(): lax.dynamic_update_slice_in_dim(full, x, (here - far) % ways * turn, axis=1)]
  transfers between devices with their start and end apart: 2 -> 4, of which waited for: 2 -> 3; matrix products, arithmetic and copies ran while one was open for 0% -> 4% of each run, Pallas kernels for 0% -> 0%
where the time goes in v1:
time: 338 us; the launch traced here: 337 us
  matrix products  127 us (38%)
  waiting for transfers between devices  102 us (30%)
  local copies, waits for them, and re-layouts  90.9 us (27%)
  between operations  13.4 us (4%)
    ppermute x3, waiting for transfers between devices, shards(): x = lax.ppermute(x, 'col', [(d, (d + 1) % ways) for d in range(ways)])  102 us
    dot_general x8, matrix products, contribute(): jnp.einsum('pik,pkj->pij', taken_left, taken_right, precision=lax.Precisi...  76.2 us
    dot_general x8, matrix products, contribute(): jnp.einsum('op,pij->oij', onehot, blocks, precision=lax.Precision.HIGHEST)  50.3 us
    gather x8, local copies, waits for them, and re-layouts, contribute(): taken_right = jnp.take(right_panel, right_slot, axis=0)  29.1 us
    gather x8, local copies, waits for them, and re-layouts, contribute(): taken_left = jnp.take(left_stack, left_slot, axis=0)  28.2 us
    squeeze x8, local copies, waits for them, and re-layouts, one_row(): left_stack = lax.dynamic_index_in_dim(pieces, offset, 0, keepdims=False)[0]  10.3 us
    squeeze x8, local copies, waits for them, and re-layouts, one_row(): right_panel = right_all[offset // col_count, offset % col_count, 0]  9.53 us
  transfers between devices with their start and end apart: 4, of which 3 were waited for; matrix products, arithmetic and copies ran while one was open for 4% of the time, Pallas kernels for 0%

profile of v1, /device:TPU:0, one launch (start us, length us, event | category | flops | bytes accessed | tf_op | source)
XLA Modules:
  0.0 337.4 jit_solution(2619742474379782668)
XLA Ops:
  10.4 36.6 %collective-permute-done = f32[2,1,1,12,128,128]{5,4,3,2,1,0:T(8,128)S(1)} collective-permute-done((f32[2,1,1,12,128,128]{5,4,3,2,1,0:T(8,128)}, f32[2,1,1,12,128,128]{5,4,3,2,1,0:T(8,128)S(1)}, u32[]{:S(2)}, u32[]{:S(2)}) %collective-permute-start) | collective-permute-done | bytes 1572896 | tf_op jit(solution)/shard_map/ppermute | solution.py:37
  47.0 37.5 %collective-permute-done.1 = f32[2,1,1,12,128,128]{5,4,3,2,1,0:T(8,128)} collective-permute-done((f32[2,1,1,12,128,128]{5,4,3,2,1,0:T(8,128)S(1)}, f32[2,1,1,12,128,128]{5,4,3,2,1,0:T(8,128)}, u32[]{:S(2)}, u32[]{:S(2)}) %collective-permute-start.1) | collective-permute-done | bytes 1572896 | tf_op jit(solution)/shard_map/ppermute | solution.py:37
  93.8 27.4 %collective-permute-done.2 = f32[2,1,1,12,128,128]{5,4,3,2,1,0:T(8,128)} collective-permute-done((f32[2,1,1,12,128,128]{5,4,3,2,1,0:T(8,128)}, f32[2,1,1,12,128,128]{5,4,3,2,1,0:T(8,128)}, u32[]{:S(2)}, u32[]{:S(2)}) %collective-permute-start.2) | collective-permute-done | bytes 1572896 | tf_op jit(solution)/shard_map/ppermute | solution.py:37
  124.1 205.0 %while.19 = (s32[]{:T(128)}, f32[24,128,128]{2,0,1:T(8,128)S(1)}, s32[]{:T(128)}, s32[]{:T(128)}, s32[8,96,3]{1,2,0:T(4,128)S(1)}, /*index=5*/f32[8,1,16,128,128...) while((s32[]{:T(128)}, f32[24,128,128]{2,0,1:T(8,128)S(1)}, ...), condition=%wide.region_3.4_spmd, body=%wide.region_0.3_spmd.sunk | while | flops 2872450304 | bytes 57164012 | solution.py:56
  124.2 25.6 %conditional.2 = (f32[24,128,128]{2,0,1:T(8,128)S(1)}) conditional(s32[]{:T(128)} %convert_element_type.13, f32[24,128,128]{2,0,1:T(8,128)S(1)} %get-tuple-element.574, (s32[]{:T(128)}, s32[8,96,3]{1,2,0:T(4,128)S(1)}, s32[]{:T(128)}, f32[8,1,16,128,128]{4,3,2,1,0:T(8,128)}, f32[2,4,1,12,128,128]{5,4,3,2,1,0:T(8,128)}, ...), branch_computations={%region_1.1_spmd, %region_2.2_spmd} | conditional | flops 2872450304 | bytes 57163708 | solution.py:49
  133.9 9.5 %fusion.2 = f32[96,128,128]{2,1,0:T(8,128)S(1)} fusion(f32[96,128,128]{2,1,0:T(8,128)} %gather_fusion.1, f32[96,128,128]{2,1,0:T(8,128)} %gather_fusion, pred[96]{0:T(512)(128)(4,1)S(1)} %get-tuple-element.513, pred[96]{0:T(512)(128)(4,1)S(1)} %get-tuple-element.512), kind=kOutput, calls=%fused_computation.4 | convolution fusion | flops 2419064832 | bytes 18874560 | tf_op jit(solution)/shard_map/while/body/eval_jaxpr/cond/branch_1_fun/pik,pkj->pij/dot_general | solution.py:16
  149.8 25.6 %conditional.2 = (f32[24,128,128]{2,0,1:T(8,128)S(1)}) conditional(s32[]{:T(128)} %convert_element_type.13, f32[24,128,128]{2,0,1:T(8,128)S(1)} %get-tuple-element.574, (s32[]{:T(128)}, s32[8,96,3]{1,2,0:T(4,128)S(1)}, s32[]{:T(128)}, f32[8,1,16,128,128]{4,3,2,1,0:T(8,128)}, f32[2,4,1,12,128,128]{5,4,3,2,1,0:T(8,128)}, ...), branch_computations={%region_1.1_spmd, %region_2.2_spmd} | conditional | flops 2872450304 | bytes 57163708 | solution.py:49
  159.6 9.5 %fusion.2 = f32[96,128,128]{2,1,0:T(8,128)S(1)} fusion(f32[96,128,128]{2,1,0:T(8,128)} %gather_fusion.1, f32[96,128,128]{2,1,0:T(8,128)} %gather_fusion, pred[96]{0:T(512)(128)(4,1)S(1)} %get-tuple-element.513, pred[96]{0:T(512)(128)(4,1)S(1)} %get-tuple-element.512), kind=kOutput, calls=%fused_computation.4 | convolution fusion | flops 2419064832 | bytes 18874560 | tf_op jit(solution)/shard_map/while/body/eval_jaxpr/cond/branch_1_fun/pik,pkj->pij/dot_general | solution.py:16
  169.1 6.3 %fusion.8 = f32[24,128,128]{2,0,1:T(8,128)S(1)} fusion(f32[24,128,128]{2,0,1:T(8,128)S(1)} %get-tuple-element.481, f32[96,128,128]{2,1,0:T(8,128)S(1)} %fusion.2, s32[96]{0:T(128)S(1)} %get-tuple-element.514, pred[96]{0:T(512)(128)(4,1)S(1)} %get-tuple-element.511), kind=kOutput, calls=%fused_computation.10 | convolution fusion | flops 453382656 | bytes 9437664 | tf_op jit(solution)/shard_map/while/body/eval_jaxpr/cond/branch_1_fun/op,pij->oij/dot_general | solution.py:21
  175.4 25.6 %conditional.2 = (f32[24,128,128]{2,0,1:T(8,128)S(1)}) conditional(s32[]{:T(128)} %convert_element_type.13, f32[24,128,128]{2,0,1:T(8,128)S(1)} %get-tuple-element.574, (s32[]{:T(128)}, s32[8,96,3]{1,2,0:T(4,128)S(1)}, s32[]{:T(128)}, f32[8,1,16,128,128]{4,3,2,1,0:T(8,128)}, f32[2,4,1,12,128,128]{5,4,3,2,1,0:T(8,128)}, ...), branch_computations={%region_1.1_spmd, %region_2.2_spmd} | conditional | flops 2872450304 | bytes 57163708 | solution.py:49
  185.2 9.5 %fusion.2 = f32[96,128,128]{2,1,0:T(8,128)S(1)} fusion(f32[96,128,128]{2,1,0:T(8,128)} %gather_fusion.1, f32[96,128,128]{2,1,0:T(8,128)} %gather_fusion, pred[96]{0:T(512)(128)(4,1)S(1)} %get-tuple-element.513, pred[96]{0:T(512)(128)(4,1)S(1)} %get-tuple-element.512), kind=kOutput, calls=%fused_computation.4 | convolution fusion | flops 2419064832 | bytes 18874560 | tf_op jit(solution)/shard_map/while/body/eval_jaxpr/cond/branch_1_fun/pik,pkj->pij/dot_general | solution.py:16
  194.7 6.3 %fusion.8 = f32[24,128,128]{2,0,1:T(8,128)S(1)} fusion(f32[24,128,128]{2,0,1:T(8,128)S(1)} %get-tuple-element.481, f32[96,128,128]{2,1,0:T(8,128)S(1)} %fusion.2, s32[96]{0:T(128)S(1)} %get-tuple-element.514, pred[96]{0:T(512)(128)(4,1)S(1)} %get-tuple-element.511), kind=kOutput, calls=%fused_computation.10 | convolution fusion | flops 453382656 | bytes 9437664 | tf_op jit(solution)/shard_map/while/body/eval_jaxpr/cond/branch_1_fun/op,pij->oij/dot_general | solution.py:21
  201.0 25.6 %conditional.2 = (f32[24,128,128]{2,0,1:T(8,128)S(1)}) conditional(s32[]{:T(128)} %convert_element_type.13, f32[24,128,128]{2,0,1:T(8,128)S(1)} %get-tuple-element.574, (s32[]{:T(128)}, s32[8,96,3]{1,2,0:T(4,128)S(1)}, s32[]{:T(128)}, f32[8,1,16,128,128]{4,3,2,1,0:T(8,128)}, f32[2,4,1,12,128,128]{5,4,3,2,1,0:T(8,128)}, ...), branch_computations={%region_1.1_spmd, %region_2.2_spmd} | conditional | flops 2872450304 | bytes 57163708 | solution.py:49
  210.8 9.5 %fusion.2 = f32[96,128,128]{2,1,0:T(8,128)S(1)} fusion(f32[96,128,128]{2,1,0:T(8,128)} %gather_fusion.1, f32[96,128,128]{2,1,0:T(8,128)} %gather_fusion, pred[96]{0:T(512)(128)(4,1)S(1)} %get-tuple-element.513, pred[96]{0:T(512)(128)(4,1)S(1)} %get-tuple-element.512), kind=kOutput, calls=%fused_computation.4 | convolution fusion | flops 2419064832 | bytes 18874560 | tf_op jit(solution)/shard_map/while/body/eval_jaxpr/cond/branch_1_fun/pik,pkj->pij/dot_general | solution.py:16
  220.3 6.3 %fusion.8 = f32[24,128,128]{2,0,1:T(8,128)S(1)} fusion(f32[24,128,128]{2,0,1:T(8,128)S(1)} %get-tuple-element.481, f32[96,128,128]{2,1,0:T(8,128)S(1)} %fusion.2, s32[96]{0:T(128)S(1)} %get-tuple-element.514, pred[96]{0:T(512)(128)(4,1)S(1)} %get-tuple-element.511), kind=kOutput, calls=%fused_computation.10 | convolution fusion | flops 453382656 | bytes 9437664 | tf_op jit(solution)/shard_map/while/body/eval_jaxpr/cond/branch_1_fun/op,pij->oij/dot_general | solution.py:21
  226.7 25.6 %conditional.2 = (f32[24,128,128]{2,0,1:T(8,128)S(1)}) conditional(s32[]{:T(128)} %convert_element_type.13, f32[24,128,128]{2,0,1:T(8,128)S(1)} %get-tuple-element.574, (s32[]{:T(128)}, s32[8,96,3]{1,2,0:T(4,128)S(1)}, s32[]{:T(128)}, f32[8,1,16,128,128]{4,3,2,1,0:T(8,128)}, f32[2,4,1,12,128,128]{5,4,3,2,1,0:T(8,128)}, ...), branch_computations={%region_1.1_spmd, %region_2.2_spmd} | conditional | flops 2872450304 | bytes 57163708 | solution.py:49
  236.4 9.5 %fusion.2 = f32[96,128,128]{2,1,0:T(8,128)S(1)} fusion(f32[96,128,128]{2,1,0:T(8,128)} %gather_fusion.1, f32[96,128,128]{2,1,0:T(8,128)} %gather_fusion, pred[96]{0:T(512)(128)(4,1)S(1)} %get-tuple-element.513, pred[96]{0:T(512)(128)(4,1)S(1)} %get-tuple-element.512), kind=kOutput, calls=%fused_computation.4 | convolution fusion | flops 2419064832 | bytes 18874560 | tf_op jit(solution)/shard_map/while/body/eval_jaxpr/cond/branch_1_fun/pik,pkj->pij/dot_general | solution.py:16
  246.0 6.3 %fusion.8 = f32[24,128,128]{2,0,1:T(8,128)S(1)} fusion(f32[24,128,128]{2,0,1:T(8,128)S(1)} %get-tuple-element.481, f32[96,128,128]{2,1,0:T(8,128)S(1)} %fusion.2, s32[96]{0:T(128)S(1)} %get-tuple-element.514, pred[96]{0:T(512)(128)(4,1)S(1)} %get-tuple-element.511), kind=kOutput, calls=%fused_computation.10 | convolution fusion | flops 453382656 | bytes 9437664 | tf_op jit(solution)/shard_map/while/body/eval_jaxpr/cond/branch_1_fun/op,pij->oij/dot_general | solution.py:21
  252.3 25.6 %conditional.2 = (f32[24,128,128]{2,0,1:T(8,128)S(1)}) conditional(s32[]{:T(128)} %convert_element_type.13, f32[24,128,128]{2,0,1:T(8,128)S(1)} %get-tuple-element.574, (s32[]{:T(128)}, s32[8,96,3]{1,2,0:T(4,128)S(1)}, s32[]{:T(128)}, f32[8,1,16,128,128]{4,3,2,1,0:T(8,128)}, f32[2,4,1,12,128,128]{5,4,3,2,1,0:T(8,128)}, ...), branch_computations={%region_1.1_spmd, %region_2.2_spmd} | conditional | flops 2872450304 | bytes 57163708 | solution.py:49
  262.0 9.5 %fusion.2 = f32[96,128,128]{2,1,0:T(8,128)S(1)} fusion(f32[96,128,128]{2,1,0:T(8,128)} %gather_fusion.1, f32[96,128,128]{2,1,0:T(8,128)} %gather_fusion, pred[96]{0:T(512)(128)(4,1)S(1)} %get-tuple-element.513, pred[96]{0:T(512)(128)(4,1)S(1)} %get-tuple-element.512), kind=kOutput, calls=%fused_computation.4 | convolution fusion | flops 2419064832 | bytes 18874560 | tf_op jit(solution)/shard_map/while/body/eval_jaxpr/cond/branch_1_fun/pik,pkj->pij/dot_general | solution.py:16
  277.9 25.6 %conditional.2 = (f32[24,128,128]{2,0,1:T(8,128)S(1)}) conditional(s32[]{:T(128)} %convert_element_type.13, f32[24,128,128]{2,0,1:T(8,128)S(1)} %get-tuple-element.574, (s32[]{:T(128)}, s32[8,96,3]{1,2,0:T(4,128)S(1)}, s32[]{:T(128)}, f32[8,1,16,128,128]{4,3,2,1,0:T(8,128)}, f32[2,4,1,12,128,128]{5,4,3,2,1,0:T(8,128)}, ...), branch_computations={%region_1.1_spmd, %region_2.2_spmd} | conditional | flops 2872450304 | bytes 57163708 | solution.py:49
  287.7 9.5 %fusion.2 = f32[96,128,128]{2,1,0:T(8,128)S(1)} fusion(f32[96,128,128]{2,1,0:T(8,128)} %gather_fusion.1, f32[96,128,128]{2,1,0:T(8,128)} %gather_fusion, pred[96]{0:T(512)(128)(4,1)S(1)} %get-tuple-element.513, pred[96]{0:T(512)(128)(4,1)S(1)} %get-tuple-element.512), kind=kOutput, calls=%fused_computation.4 | convolution fusion | flops 2419064832 | bytes 18874560 | tf_op jit(solution)/shard_map/while/body/eval_jaxpr/cond/branch_1_fun/pik,pkj->pij/dot_general | solution.py:16
  303.5 25.6 %conditional.2 = (f32[24,128,128]{2,0,1:T(8,128)S(1)}) conditional(s32[]{:T(128)} %convert_element_type.13, f32[24,128,128]{2,0,1:T(8,128)S(1)} %get-tuple-element.574, (s32[]{:T(128)}, s32[8,96,3]{1,2,0:T(4,128)S(1)}, s32[]{:T(128)}, f32[8,1,16,128,128]{4,3,2,1,0:T(8,128)}, f32[2,4,1,12,128,128]{5,4,3,2,1,0:T(8,128)}, ...), branch_computations={%region_1.1_spmd, %region_2.2_spmd} | conditional | flops 2872450304 | bytes 57163708 | solution.py:49
  313.3 9.5 %fusion.2 = f32[96,128,128]{2,1,0:T(8,128)S(1)} fusion(f32[96,128,128]{2,1,0:T(8,128)} %gather_fusion.1, f32[96,128,128]{2,1,0:T(8,128)} %gather_fusion, pred[96]{0:T(512)(128)(4,1)S(1)} %get-tuple-element.513, pred[96]{0:T(512)(128)(4,1)S(1)} %get-tuple-element.512), kind=kOutput, calls=%fused_computation.4 | convolution fusion | flops 2419064832 | bytes 18874560 | tf_op jit(solution)/shard_map/while/body/eval_jaxpr/cond/branch_1_fun/pik,pkj->pij/dot_general | solution.py:16
  (84 shorter events, 120.0 us)
Async XLA Ops:
  6.5 82.1 %copy-start = (f32[2,1,1,12,128,128]{5,4,3,2,1,0:T(8,128)S(1)}, f32[2,1,1,12,128,128]{5,4,3,2,1,0:T(8,128)}, u32[]{:S(2)}) copy-start(f32[2,1,1,12,128,128]{5,4,3,2,1,0:T(8,128)} %param.8) | copy-start | bytes 4718596
  6.5 117.5 %all-gather.2.cloned.1.call-start = ((), (), s32[]{:S(2)}) async-start(), calls=%async_computation | async-start | bytes 9437184 | tf_op jit(solution)/shard_map/all_gather | solution.py:40
  7.3 39.7 %collective-permute-start = (f32[2,1,1,12,128,128]{5,4,3,2,1,0:T(8,128)}, f32[2,1,1,12,128,128]{5,4,3,2,1,0:T(8,128)S(1)}, u32[]{:S(2)}, u32[]{:S(2)}) collective-permute-start(f32[2,1,1,12,128,128]{5,4,3,2,1,0:T(8,128)} %param.8), channel_id=1, source_target_pairs={{0,1},{1,2},{2,3},{3,0},{4,5},{5,6},{6,7},{7,4},{8,9},{9,10},{10,1... | collective-permute-start | bytes 4718600 | tf_op jit(solution)/shard_map/ppermute | solution.py:37
  47.0 37.5 %collective-permute-start.1 = (f32[2,1,1,12,128,128]{5,4,3,2,1,0:T(8,128)S(1)}, f32[2,1,1,12,128,128]{5,4,3,2,1,0:T(8,128)}, u32[]{:S(2)}, u32[]{:S(2)}) collective-permute-start(f32[2,1,1,12,128,128]{5,4,3,2,1,0:T(8,128)S(1)} %collective-permute-done), channel_id=1, source_target_pairs={{0,1},{1,2},{2,3},{3,0},{4,5},{5,6},{6,7},{7,4},{8,9},{9,10},{10,1... | collective-permute-start | bytes 4718600 | tf_op jit(solution)/shard_map/ppermute | solution.py:37
  84.5 36.8 %collective-permute-start.2 = (f32[2,1,1,12,128,128]{5,4,3,2,1,0:T(8,128)}, f32[2,1,1,12,128,128]{5,4,3,2,1,0:T(8,128)}, u32[]{:S(2)}, u32[]{:S(2)}) collective-permute-start(f32[2,1,1,12,128,128]{5,4,3,2,1,0:T(8,128)} %collective-permute-done.1), channel_id=1, source_target_pairs={{0,1},{1,2},{2,3},{3,0},{4,5},{5,6},{6,7},{7,4},{8,9},{9,10},{10,1... | collective-permute-start | bytes 4718600 | tf_op jit(solution)/shard_map/ppermute | solution.py:37
Sparse Core Ops, SparseCore 0:
  9.2 56.9 all-gather.1
